TPU v7x, 32 devices: a whole 2x2x4 slice. The times are simulated.
32 devices in a mesh: win: 2 (over y), px: 16 (over z, x, core).
Axes of the slice: x: 2, y: 2, z: 4, core: 2. Of those that a mesh axis runs over, the one named last changes fastest.
Arguments:
- charge_a: float32 [131072], P(('win', 'px')), parts along dimension 0, may hold values from -3 to 3
- charge_b: float32 [131072], P(('win', 'px')), parts along dimension 0, may hold values from -3 to 3
- coupling: float32 [2], P('win'), parts along dimension 0, may hold values from 0.1 to 0.9
- positions: float32 [3, 131072], P(None, ('win', 'px')), parts along dimension 1, may hold values from 0 to 128, as said below
- grid_base: int32 [3, 131072], P(None, ('win', 'px')), parts along dimension 1, may hold values from 0 to 127, as said below
- spline: float32 [3, 4, 131072], P(None, None, ('win', 'px')), parts along dimension 2, may hold values from 0 to 0.67, as said below
- spline_slope: float32 [3, 4, 131072], P(None, None, ('win', 'px')), parts along dimension 2, may hold values from -0.67 to 0.67, as said below
- influence: float32 [128, 128, 128], P(None, 'px'), may hold values from 0.5 to 300, as said below
- pair_tiles: int32 [1024, 12], P(('win', 'px')), parts along dimension 0, may hold values from 0 to 39
- ghost_lists: int32 [2, 16384], P(None, ('win', 'px')), parts along dimension 1, may hold values from 0 to 4095
Outputs:
- forces: float32 [3, 131072], P(None, ('win', 'px')), parts along dimension 1
There are 2 independent parts, one for each index of `win`. A program takes and returns all parts, laid end to end along the dimension named above; an argument that names none is the same for every part. Nothing has to cross between parts.
Inputs may be any that keep to these rules, and one draw needn't show every extreme that they name: `grid_base`: row 0 of atom i lies in [d * 8, (d + 1) * 8) for d = i // 4096; rows 1 and 2 lie in [0, 128). `positions`: row 0 of atom i lies in [d * 8, (d + 1) * 8) for d = i // 4096; rows 1 and 2 lie in [0, 8). For each atom and dimension, the 4 cubic B-spline weights at some fraction u in [0, 1). `spline_slope`: the derivatives in u of the weights in spline, at the same u. influence at wave index m equals influence at -m, indices taken modulo the grid's lengths.
All inputs are finite; a program needn't handle non-finite values.
Results may differ from a plain program's by a relative error of at most 0.0003.
Values sent between devices are 32-bit elements; how exact they have to be, the bound alone decides.
A program may use at most 256 MiB of HBM per device.

v0:
```python
import math

import jax
import jax.numpy as jnp
from jax import lax
from jax.sharding import PartitionSpec as P

TILE = 128


highest = lax.Precision.HIGHEST
ewald_beta = 0.35
soften_sq = 0.25


def from_behind(value, axis, steps):
    count = lax.axis_size(axis)
    pairs = [(source, (source + steps) % count) for source in range(count)]
    return lax.ppermute(value, axis, pairs)


def dft_tables(length):
    wave_index = jnp.arange(length, dtype=jnp.int32)
    phase_angle = (
        2.0
        * math.pi
        / length
        * (wave_index[:, None] * wave_index[None, :] % length).astype(jnp.float32)
    )
    return (jnp.cos(phase_angle), jnp.sin(phase_angle))


def along_axis(values, matrix, dim_index):
    result = jnp.tensordot(values, matrix, axes=([dim_index], [0]), precision=highest)
    return jnp.moveaxis(result, -1, dim_index)


def transform(real_part, imag_part, dim_index, forward):
    cosine_table, sine_table = dft_tables(real_part.shape[dim_index])
    factor = 1.0 if forward else -1.0
    real_cos = along_axis(real_part, cosine_table, dim_index)
    real_new = real_cos + factor * along_axis(imag_part, sine_table, dim_index)
    imag_new = along_axis(imag_part, cosine_table, dim_index) - factor * along_axis(
        real_part, sine_table, dim_index
    )
    return (real_new, imag_new)


def spline_rows(base_index, weights, length, periodic):
    cell_ids = jnp.arange(length, dtype=jnp.int32)
    result = jnp.zeros((base_index.shape[0], length), jnp.float32)
    for offset in range(weights.shape[0]):
        target_cell = base_index + offset
        if periodic:
            target_cell = target_cell % length
        result = result + jnp.where(
            target_cell[:, None] == cell_ids[None, :], weights[offset][:, None], 0.0
        )
    return result


def pair_block(home_rows, nearby, weight_b):
    separation = home_rows[0:3, :, :, None] - nearby[0:3, :, None, :]
    dist_sq = jnp.sum(separation * separation, axis=0) + soften_sq
    distance = jnp.sqrt(dist_sq)
    radial = (
        jax.scipy.special.erfc(ewald_beta * distance) / distance
        + 2.0 * ewald_beta / math.sqrt(math.pi) * jnp.exp(-ewald_beta * ewald_beta * dist_sq)
    ) / dist_sq
    mixed = (1.0 - weight_b) * home_rows[3][:, :, None] * nearby[3][
        :, None, :
    ] + weight_b * home_rows[4][:, :, None] * nearby[4][:, None, :]
    return jnp.sum((mixed * radial)[None] * separation, axis=3)


def device_pairs(home_rows, candidates, tile_list, weight_b):
    home_tiles = home_rows.reshape(5, -1, TILE)
    cand_tiles = candidates.reshape(5, -1, TILE)

    def one_slot(accumulated, column):
        nearby = jnp.take(cand_tiles, column, axis=1)
        return (accumulated + pair_block(home_tiles, nearby, weight_b), None)

    start = jnp.zeros((3,) + home_tiles.shape[1:], jnp.float32)
    accumulated, unused = lax.scan(one_slot, start, tile_list.T)
    return accumulated.reshape(3, -1)


def per_device(
    charge_a,
    charge_b,
    coupling,
    positions,
    grid_base,
    spline,
    spline_slope,
    influence,
    pair_tiles,
    ghost_lists,
):
    group_size = lax.axis_size("px")
    me_index = lax.axis_index("px")
    atom_count = charge_a.shape[0]
    full_x, slab_y, full_z = influence.shape
    full_y = slab_y * group_size
    planes = full_x // group_size
    margin = spline.shape[1] - 1
    slab_width = planes + margin
    hop_count = (margin + planes - 1) // planes
    weight_b = coupling[0]
    local_x = grid_base[0] - me_index * planes
    rows_x = spline_rows(local_x, spline[0], slab_width, False)
    slope_x = spline_rows(local_x, spline_slope[0], slab_width, False)
    rows_y = spline_rows(grid_base[1], spline[1], full_y, True)
    slope_y = spline_rows(grid_base[1], spline_slope[1], full_y, True)
    rows_z = spline_rows(grid_base[2], spline[2], full_z, True)
    slope_z = spline_rows(grid_base[2], spline_slope[2], full_z, True)
    lifted = (rows_x[:, :, None] * rows_y[:, None, :]).reshape(atom_count, slab_width * full_y)
    lifted = jnp.concatenate([charge_a[:, None] * lifted, charge_b[:, None] * lifted], axis=1)
    spread = jnp.einsum("ar,az->rz", lifted, rows_z, precision=highest).reshape(
        2, slab_width, full_y, full_z
    )
    owned_grid = spread[:, :planes]
    for distance in range(1, hop_count + 1):
        first_layer = (distance - 1) * planes
        last_layer = min(distance * planes, margin)
        arrived = from_behind(spread[:, planes + first_layer : planes + last_layer], "px", distance)
        owned_grid = owned_grid.at[:, : last_layer - first_layer].add(arrived)
    real_part, imag_part = transform(owned_grid[0:1], owned_grid[1:2], 3, True)
    real_part, imag_part = transform(real_part, imag_part, 2, True)
    channels = real_part.shape[0]
    stacked = jnp.concatenate([real_part, imag_part], axis=0)
    columns = lax.all_to_all(stacked, "px", split_axis=2, concat_axis=1, tiled=True)
    real_part, imag_part = transform(columns[:channels], columns[channels:], 1, True)
    real_part = real_part * influence[None]
    imag_part = imag_part * influence[None]
    real_part, imag_part = transform(real_part, imag_part, 1, False)
    stacked = jnp.concatenate([real_part, imag_part], axis=0)
    returned = lax.all_to_all(stacked, "px", split_axis=1, concat_axis=2, tiled=True)
    real_part, imag_part = transform(returned[:channels], returned[channels:], 2, False)
    inverse_scale = 1.0 / (full_x * full_y * full_z)
    real_part, imag_part = transform(real_part, imag_part, 3, False)
    potential = jnp.concatenate([real_part, imag_part], axis=0) * inverse_scale
    pieces = [potential]
    for distance in range(1, hop_count + 1):
        first_layer = (distance - 1) * planes
        last_layer = min(distance * planes, margin)
        pieces.append(from_behind(potential[:, : last_layer - first_layer], "px", -distance))
    potential = jnp.concatenate(pieces, axis=1)
    stacked_z = jnp.concatenate([rows_z, slope_z], axis=0)
    sampled = jnp.einsum(
        "az,rz->ar",
        stacked_z,
        potential.reshape(2 * slab_width * full_y, full_z),
        precision=highest,
    )
    sampled = sampled.reshape(2, atom_count, 2, slab_width, full_y)
    plain_z = sampled[0]
    slope_zed = sampled[1]
    along_y = jnp.einsum("aspy,ay->asp", plain_z, rows_y, precision=highest)
    slope_along_y = jnp.einsum("aspy,ay->asp", plain_z, slope_y, precision=highest)
    zed_along_y = jnp.einsum("aspy,ay->asp", slope_zed, rows_y, precision=highest)
    grad_x = jnp.einsum("asp,ap->sa", along_y, slope_x, precision=highest)
    grad_y = jnp.einsum("asp,ap->sa", slope_along_y, rows_x, precision=highest)
    grad_z = jnp.einsum("asp,ap->sa", zed_along_y, rows_x, precision=highest)
    gradient = jnp.stack([grad_x, grad_y, grad_z])
    reciprocal = -(
        (1.0 - weight_b) * charge_a * gradient[:, 0] + weight_b * charge_b * gradient[:, 1]
    )
    packet = jnp.concatenate([positions, charge_a[None], charge_b[None]], axis=0)
    to_right = jnp.take(packet, ghost_lists[0], axis=1)
    to_left = jnp.take(packet, ghost_lists[1], axis=1)
    from_left = from_behind(to_right, "px", 1)
    from_right = from_behind(to_left, "px", -1)
    from_left = from_left.at[0].add(jnp.where(me_index == 0, -float(full_x), 0.0))
    from_right = from_right.at[0].add(jnp.where(me_index == group_size - 1, float(full_x), 0.0))
    candidates = jnp.concatenate([packet, from_left, from_right], axis=1)
    real_space = device_pairs(packet, candidates, pair_tiles, weight_b)
    return reciprocal + real_space


def solution(mesh):
    placed = (
        P(("win", "px")),
        P(("win", "px")),
        P("win"),
        P(None, ("win", "px")),
        P(None, ("win", "px")),
        P(None, None, ("win", "px")),
        P(None, None, ("win", "px")),
        P(None, "px", None),
        P(("win", "px"), None),
        P(None, ("win", "px")),
    )
    return jax.shard_map(
        per_device, mesh=mesh, in_specs=placed, out_specs=P(None, ("win", "px")), check_vma=False
    )
```

profile of v0, /device:TPU:20, one launch (start us, length us, event | category | flops | bytes accessed | tf_op | source)
XLA Modules:
  0.0 542.2 jit_solution(716740211092543806)
XLA Ops:
  0.0 1.5 fusion.239
  1.5 1.5 fusion.238
  4.9 2.5 select_add_fusion.1
  7.5 10.6 %broadcast_multiply_fusion = f32[4096,11,128]{0,2,1:T(8,128)} fusion(f32[4096,128]{0,1:T(8,128)S(1)} %get-tuple-element.228, f32[4096,11]{0,1:T(8,128)S(1)} %get-tuple-element.226), kind=kLoop, calls=%fused_computation.48 | loop fusion | flops 5767168 | bytes 25346048 | tf_op jit(solution)/shard_map/mul | solution.py:118
  18.0 17.1 %bitcast_multiply_fusion.1 = (f32[4096,1408]{0,1:T(8,128)S(1)}, f32[4096,1408]{0,1:T(8,128)}) fusion(f32[4096,11,128]{0,2,1:T(8,128)} %broadcast_multiply_fusion, f32[4096]{0:T(1024)S(1)} %copy-done.14, f32[4096]{0:T(1024)S(1)} %copy-done.13), kind=kLoop, calls=%fused_computation.47 | loop fusion | flops 11534336 | bytes 69238784 | tf_op jit(solution)/shard_map/mul | solution.py:119
  35.1 41.3 %fusion.16 = f32[2816,128]{1,0:T(8,128)S(1)} fusion(f32[4096,1408]{0,1:T(8,128)} %get-tuple-element.196, f32[4096,1408]{0,1:T(8,128)S(1)} %get-tuple-element.195, f32[4096]{0:T(1024)S(1)} %bitcast.304, s32[4096]{0:T(1024)S(1)} %get-tuple-element.237, f32[4096]{0:T(1024)S(1)} %bitcast.306, s32[4096]{0:T(1024)S(1)} %get-tuple-element.236, ...), kind=kOutput, calls=%fused_computation.39 | convolution fusion | flops 17734041600 | bytes 47710208 | tf_op jit(solution)/shard_map/ar,az->rz/dot_general | solution.py:120
  76.8 8.0 %collective-permute-done = f32[2,3,128,128]{3,2,1,0:T(8,128)S(1)} collective-permute-done((f32[2,3,128,128]{3,2,1,0:T(8,128)S(1)}, f32[2,3,128,128]{3,2,1,0:T(8,128)S(1)}, u32[]{:S(2)}, u32[]{:S(2)}) %collective-permute-start) | collective-permute-done | bytes 393248 | tf_op jit(solution)/shard_map/ppermute | solution.py:19
  92.8 1.4 copy.152
  94.2 5.6 %all-to-all-start = ((f32[2,8,128,128]{3,1,0,2:T(8,128)}), f32[2,8,128,128]{3,1,0,2:T(8,128)S(1)}, u32[]{:S(2)}, u32[]{:S(2)}) async-start(f32[2,8,128,128]{3,1,0,2:T(8,128)} %copy.152), calls=%async_computation | async-start | bytes 2097152 | tf_op jit(solution)/shard_map/all_to_all | solution.py:133
  101.3 1.6 gather_fusion.1
  102.9 1.8 select_bitcast_fusion.2
  105.2 1.2 copy.158
  106.5 3.2 gather_fusion.2
  110.2 15.3 %all-to-all-done = f32[2,8,128,128]{3,1,0,2:T(8,128)S(1)} async-done(((f32[2,8,128,128]{3,1,0,2:T(8,128)}), f32[2,8,128,128]{3,1,0,2:T(8,128)S(1)}, u32[]{:S(2)}, u32[]{:S(2)}) %all-to-all-start) | async-done | bytes 1048608 | tf_op jit(solution)/shard_map/all_to_all | solution.py:133
  133.2 1.4 copy.161
  134.6 6.0 %all-to-all-start.1 = ((f32[2,128,8,128]{3,2,0,1:T(8,128)}), f32[2,128,8,128]{3,2,0,1:T(8,128)S(1)}, u32[]{:S(2)}, u32[]{:S(2)}) async-start(f32[2,128,8,128]{3,2,0,1:T(8,128)} %copy.161), calls=%async_computation.1 | async-start | bytes 2097152 | tf_op jit(solution)/shard_map/all_to_all | solution.py:139
  143.9 2.6 select_add_fusion.4
  146.5 1.7 slice_add_fusion.2
  148.2 1.7 scatter-add.11
  151.0 15.8 %collective-permute-done.3 = f32[5,512]{0,1:T(8,128)} collective-permute-done((f32[5,512]{0,1:T(8,128)}, f32[5,512]{0,1:T(8,128)}, u32[]{:S(2)}, u32[]{:S(2)}) %collective-permute-start.3) | collective-permute-done | bytes 10272 | tf_op jit(solution)/shard_map/ppermute | solution.py:19
  166.8 1.7 slice_add_fusion.1
  168.4 1.9 scatter-add.14
  181.7 2.8 collective-permute-start.1
  184.5 183.1 %while.15 = (s32[]{:T(128)}, f32[3,32,128]{2,1,0:T(8,128)}, f32[]{:T(128)}, f32[5,32,128]{2,1,0:T(8,128)S(1)}, s32[12,32]{1,0:T(8,128)}, /*index=5*/f32[5,40,128]{2,0,1:T(8,128)S(1)}, f32[]{:T(128)}, s32[]{:T(128)}, s32[]{:T(128)}) while((s32[]{:T(128)}, f32[3,32,128]{2,1,0:T(8,128)}, f32[]{:T(128)}, f32[5,32,128]{2,1,0:T(8,128)S(1)}, ...), condition=%wide.region_3.5_spmd.clone, body=%wide.region_0.4_spmd.clone.sunk | while | flops 46179616 | bytes 9999215 | solution.py:85
  186.6 2.1 fusion.268
  189.4 5.8 %fusion.270 = f32[32,128,128]{2,1,0:T(8,128)S(1)} fusion(f32[32,128,128]{2,1,0:T(8,128)S(1)} %fusion.268, f32[32,128]{1,0:T(8,128)S(1)} %bitcast.288, f32[32,128]{1,0:T(8,128)S(1)} %get-tuple-element.298, f32[32,128]{1,0:T(8,128)S(1)} %bitcast.287, f32[32,128]{1,0:T(8,128)S(1)} %get-tuple-element.300), kind=kLoop, calls=%fused_computation.12.clone.1 | loop fusion | flops 37224448 | bytes 4259840 | tf_op jit(solution)/shard_map/while/body/eval_jaxpr/mul | solution.py:73
  195.2 3.8 fusion.271
  201.9 2.1 fusion.268
  204.6 5.8 %fusion.270 = f32[32,128,128]{2,1,0:T(8,128)S(1)} fusion(f32[32,128,128]{2,1,0:T(8,128)S(1)} %fusion.268, f32[32,128]{1,0:T(8,128)S(1)} %bitcast.288, f32[32,128]{1,0:T(8,128)S(1)} %get-tuple-element.298, f32[32,128]{1,0:T(8,128)S(1)} %bitcast.287, f32[32,128]{1,0:T(8,128)S(1)} %get-tuple-element.300), kind=kLoop, calls=%fused_computation.12.clone.1 | loop fusion | flops 37224448 | bytes 4259840 | tf_op jit(solution)/shard_map/while/body/eval_jaxpr/mul | solution.py:73
  210.5 3.8 fusion.271
  217.1 2.1 fusion.268
  219.9 5.8 %fusion.270 = f32[32,128,128]{2,1,0:T(8,128)S(1)} fusion(f32[32,128,128]{2,1,0:T(8,128)S(1)} %fusion.268, f32[32,128]{1,0:T(8,128)S(1)} %bitcast.288, f32[32,128]{1,0:T(8,128)S(1)} %get-tuple-element.298, f32[32,128]{1,0:T(8,128)S(1)} %bitcast.287, f32[32,128]{1,0:T(8,128)S(1)} %get-tuple-element.300), kind=kLoop, calls=%fused_computation.12.clone.1 | loop fusion | flops 37224448 | bytes 4259840 | tf_op jit(solution)/shard_map/while/body/eval_jaxpr/mul | solution.py:73
  225.7 3.8 fusion.271
  232.4 2.1 fusion.268
  235.2 5.8 %fusion.270 = f32[32,128,128]{2,1,0:T(8,128)S(1)} fusion(f32[32,128,128]{2,1,0:T(8,128)S(1)} %fusion.268, f32[32,128]{1,0:T(8,128)S(1)} %bitcast.288, f32[32,128]{1,0:T(8,128)S(1)} %get-tuple-element.298, f32[32,128]{1,0:T(8,128)S(1)} %bitcast.287, f32[32,128]{1,0:T(8,128)S(1)} %get-tuple-element.300), kind=kLoop, calls=%fused_computation.12.clone.1 | loop fusion | flops 37224448 | bytes 4259840 | tf_op jit(solution)/shard_map/while/body/eval_jaxpr/mul | solution.py:73
  241.0 3.8 fusion.271
  247.6 2.1 fusion.268
  250.4 5.8 %fusion.270 = f32[32,128,128]{2,1,0:T(8,128)S(1)} fusion(f32[32,128,128]{2,1,0:T(8,128)S(1)} %fusion.268, f32[32,128]{1,0:T(8,128)S(1)} %bitcast.288, f32[32,128]{1,0:T(8,128)S(1)} %get-tuple-element.298, f32[32,128]{1,0:T(8,128)S(1)} %bitcast.287, f32[32,128]{1,0:T(8,128)S(1)} %get-tuple-element.300), kind=kLoop, calls=%fused_computation.12.clone.1 | loop fusion | flops 37224448 | bytes 4259840 | tf_op jit(solution)/shard_map/while/body/eval_jaxpr/mul | solution.py:73
  256.3 3.8 fusion.271
  262.9 2.1 fusion.268
  265.7 5.8 %fusion.270 = f32[32,128,128]{2,1,0:T(8,128)S(1)} fusion(f32[32,128,128]{2,1,0:T(8,128)S(1)} %fusion.268, f32[32,128]{1,0:T(8,128)S(1)} %bitcast.288, f32[32,128]{1,0:T(8,128)S(1)} %get-tuple-element.298, f32[32,128]{1,0:T(8,128)S(1)} %bitcast.287, f32[32,128]{1,0:T(8,128)S(1)} %get-tuple-element.300), kind=kLoop, calls=%fused_computation.12.clone.1 | loop fusion | flops 37224448 | bytes 4259840 | tf_op jit(solution)/shard_map/while/body/eval_jaxpr/mul | solution.py:73
  271.5 3.8 fusion.271
  278.1 2.1 fusion.268
  280.9 5.8 %fusion.270 = f32[32,128,128]{2,1,0:T(8,128)S(1)} fusion(f32[32,128,128]{2,1,0:T(8,128)S(1)} %fusion.268, f32[32,128]{1,0:T(8,128)S(1)} %bitcast.288, f32[32,128]{1,0:T(8,128)S(1)} %get-tuple-element.298, f32[32,128]{1,0:T(8,128)S(1)} %bitcast.287, f32[32,128]{1,0:T(8,128)S(1)} %get-tuple-element.300), kind=kLoop, calls=%fused_computation.12.clone.1 | loop fusion | flops 37224448 | bytes 4259840 | tf_op jit(solution)/shard_map/while/body/eval_jaxpr/mul | solution.py:73
  286.8 3.8 fusion.271
  293.4 2.1 fusion.268
  296.2 5.8 %fusion.270 = f32[32,128,128]{2,1,0:T(8,128)S(1)} fusion(f32[32,128,128]{2,1,0:T(8,128)S(1)} %fusion.268, f32[32,128]{1,0:T(8,128)S(1)} %bitcast.288, f32[32,128]{1,0:T(8,128)S(1)} %get-tuple-element.298, f32[32,128]{1,0:T(8,128)S(1)} %bitcast.287, f32[32,128]{1,0:T(8,128)S(1)} %get-tuple-element.300), kind=kLoop, calls=%fused_computation.12.clone.1 | loop fusion | flops 37224448 | bytes 4259840 | tf_op jit(solution)/shard_map/while/body/eval_jaxpr/mul | solution.py:73
  302.0 3.8 fusion.271
  308.7 2.1 fusion.268
  311.4 5.8 %fusion.270 = f32[32,128,128]{2,1,0:T(8,128)S(1)} fusion(f32[32,128,128]{2,1,0:T(8,128)S(1)} %fusion.268, f32[32,128]{1,0:T(8,128)S(1)} %bitcast.288, f32[32,128]{1,0:T(8,128)S(1)} %get-tuple-element.298, f32[32,128]{1,0:T(8,128)S(1)} %bitcast.287, f32[32,128]{1,0:T(8,128)S(1)} %get-tuple-element.300), kind=kLoop, calls=%fused_computation.12.clone.1 | loop fusion | flops 37224448 | bytes 4259840 | tf_op jit(solution)/shard_map/while/body/eval_jaxpr/mul | solution.py:73
  317.3 3.8 fusion.271
  323.9 2.1 fusion.268
  326.7 5.8 %fusion.270 = f32[32,128,128]{2,1,0:T(8,128)S(1)} fusion(f32[32,128,128]{2,1,0:T(8,128)S(1)} %fusion.268, f32[32,128]{1,0:T(8,128)S(1)} %bitcast.288, f32[32,128]{1,0:T(8,128)S(1)} %get-tuple-element.298, f32[32,128]{1,0:T(8,128)S(1)} %bitcast.287, f32[32,128]{1,0:T(8,128)S(1)} %get-tuple-element.300), kind=kLoop, calls=%fused_computation.12.clone.1 | loop fusion | flops 37224448 | bytes 4259840 | tf_op jit(solution)/shard_map/while/body/eval_jaxpr/mul | solution.py:73
  332.5 3.8 fusion.271
  339.2 2.1 fusion.268
  341.9 5.8 %fusion.270 = f32[32,128,128]{2,1,0:T(8,128)S(1)} fusion(f32[32,128,128]{2,1,0:T(8,128)S(1)} %fusion.268, f32[32,128]{1,0:T(8,128)S(1)} %bitcast.288, f32[32,128]{1,0:T(8,128)S(1)} %get-tuple-element.298, f32[32,128]{1,0:T(8,128)S(1)} %bitcast.287, f32[32,128]{1,0:T(8,128)S(1)} %get-tuple-element.300), kind=kLoop, calls=%fused_computation.12.clone.1 | loop fusion | flops 37224448 | bytes 4259840 | tf_op jit(solution)/shard_map/while/body/eval_jaxpr/mul | solution.py:73
  347.8 3.8 fusion.271
  354.4 2.1 fusion.268
  357.2 5.8 %fusion.270 = f32[32,128,128]{2,1,0:T(8,128)S(1)} fusion(f32[32,128,128]{2,1,0:T(8,128)S(1)} %fusion.268, f32[32,128]{1,0:T(8,128)S(1)} %bitcast.288, f32[32,128]{1,0:T(8,128)S(1)} %get-tuple-element.298, f32[32,128]{1,0:T(8,128)S(1)} %bitcast.287, f32[32,128]{1,0:T(8,128)S(1)} %get-tuple-element.300), kind=kLoop, calls=%fused_computation.12.clone.1 | loop fusion | flops 37224448 | bytes 4259840 | tf_op jit(solution)/shard_map/while/body/eval_jaxpr/mul | solution.py:73
  363.0 3.8 fusion.271
  367.5 1.3 pad_maximum_fusion
  369.2 77.7 %fusion.20 = f32[8192,2816]{0,1:T(8,128)} fusion(f32[2816,128]{1,0:T(8,128)S(1)} %bitcast.278, f32[4096,128]{0,1:T(8,128)S(1)} %copy-done.3, f32[4096,128]{0,1:T(8,128)S(1)} %get-tuple-element.229), kind=kOutput, calls=%fused_computation.49 | convolution fusion | flops 35434528768 | bytes 97910784 | tf_op jit(solution)/shard_map/az,rz->ar/dot_general | solution.py:151
  447.0 61.4 %fusion.235 = (f32[4096,2816]{0,1:T(8,128)}, f32[4096,2816]{0,1:T(8,128)}) fusion(f32[8192,2816]{0,1:T(8,128)} %fusion.20), kind=kLoop, calls=%fused_computation.332 | loop fusion | bytes 184549376 | tf_op jit(solution)/shard_map/slice | solution.py:159
  508.4 31.3 %multiply_reduce_fusion.2 = (f32[4096,2,11]{0,2,1:T(8,128)S(1)}, f32[4096,2,11]{0,2,1:T(8,128)S(1)}, f32[4096,2,11]{0,2,1:T(8,128)S(1)}) fusion(f32[4096,128,2,11]{0,1,3,2:T(8,128)} %bitcast.277, f32[4096,128]{0,1:T(8,128)S(1)} %copy-done.1, f32[4096,128]{0,1:T(8,128)S(1)} %copy-done.2, f32[4096,128,2,11]{0,1,3,2:T(8,128)} %bitcast.276), kind=kLoop, calls=%fused_computation.45 | loop fusion | flops 68935680 | bytes 97550336
  (291 shorter events, 78.6 us)
Async XLA Ops:
  4.1 31.0 %copy-start.16 = (s32[4096]{0:T(1024)}, s32[4096]{0:T(1024)S(1)}, u32[]{:S(2)}) copy-start(s32[4096]{0:T(1024)S(1)} %get-tuple-element.237) | copy-start | bytes 49156
  4.9 2.5 copy-start.5
  7.5 10.6 %copy-start = (f32[4096,128]{0,1:T(8,128)}, f32[4096,128]{0,1:T(8,128)S(1)}, u32[]{:S(2)}) copy-start(f32[4096,128]{0,1:T(8,128)S(1)} %get-tuple-element.228) | copy-start | bytes 6291460
  7.5 10.6 %copy-start.13 = (f32[4096]{0:T(1024)S(1)}, f32[4096]{0:T(1024)}, u32[]{:S(2)}) copy-start(f32[4096]{0:T(1024)} %param.21) | copy-start | bytes 49156
  7.5 10.6 %copy-start.14 = (f32[4096]{0:T(1024)S(1)}, f32[4096]{0:T(1024)}, u32[]{:S(2)}) copy-start(f32[4096]{0:T(1024)} %param.20) | copy-start | bytes 49156
  76.4 8.4 %collective-permute-start = (f32[2,3,128,128]{3,2,1,0:T(8,128)S(1)}, f32[2,3,128,128]{3,2,1,0:T(8,128)S(1)}, u32[]{:S(2)}, u32[]{:S(2)}) collective-permute-start(f32[2,3,128,128]{3,2,1,0:T(8,128)S(1)} %slice.338), channel_id=1, source_target_pairs={{0,1},{1,2},{2,3},{3,4},{4,5},{5,6},{6,7},{7,8},{8,9},{9,10},{10,1... | collective-permute-start | bytes 1179656 | tf_op jit(solution)/shard_map/ppermute | solution.py:19
  92.8 7.0 %copy-start.11 = (f32[3,4096]{1,0:T(4,128)S(1)}, f32[3,4096]{1,0:T(4,128)}, u32[]{:S(2)}) copy-start(f32[3,4096]{1,0:T(4,128)} %param.23) | copy-start | bytes 147460
  94.2 31.4 %all-to-all-start = ((f32[2,8,128,128]{3,1,0,2:T(8,128)}), f32[2,8,128,128]{3,1,0,2:T(8,128)S(1)}, u32[]{:S(2)}, u32[]{:S(2)}) async-start(f32[2,8,128,128]{3,1,0,2:T(8,128)} %copy.152), calls=%async_computation | async-start | bytes 2097152 | tf_op jit(solution)/shard_map/all_to_all | solution.py:133
  100.5 4.2 copy-start.4
  104.7 41.8 %collective-permute-start.2 = (f32[5,512]{0,1:T(8,128)}, f32[5,512]{0,1:T(8,128)}, u32[]{:S(2)}, u32[]{:S(2)}) collective-permute-start(f32[5,512]{0,1:T(8,128)} %select_bitcast_fusion.2), channel_id=1, source_target_pairs={{0,1},{1,2},{2,3},{3,4},{4,5},{5,6},{6,7},{7,8},{8,9},{9,10},{10,1... | collective-permute-start | bytes 30728 | tf_op jit(solution)/shard_map/ppermute | solution.py:19
  133.2 7.4 %copy-start.15 = (f32[512,5]{1,0:T(8,128)S(1)}, f32[512,5]{1,0:T(8,128)}, u32[]{:S(2)}) copy-start(f32[512,5]{1,0:T(8,128)} %gather_fusion.2) | copy-start | bytes 30724
  133.2 7.4 %copy-start.20 = (pred[512]{0:T(512)(128)(4,1)S(1)}, pred[512]{0:T(512)(128)(4,1)}, u32[]{:S(2)}) copy-start(pred[512]{0:T(512)(128)(4,1)} %compare_and_fusion.1) | copy-start | bytes 1540
  134.6 9.3 %copy-start.17 = (s32[4096]{0:T(1024)S(1)}, s32[4096]{0:T(1024)}, u32[]{:S(2)}) copy-start(s32[4096]{0:T(1024)} %copy-done.16) | copy-start | bytes 49156
  134.6 36.8 %all-to-all-start.1 = ((f32[2,128,8,128]{3,2,0,1:T(8,128)}), f32[2,128,8,128]{3,2,0,1:T(8,128)S(1)}, u32[]{:S(2)}, u32[]{:S(2)}) async-start(f32[2,128,8,128]{3,2,0,1:T(8,128)} %copy.161), calls=%async_computation.1 | async-start | bytes 2097152 | tf_op jit(solution)/shard_map/all_to_all | solution.py:139
  141.5 25.3 %collective-permute-start.3 = (f32[5,512]{0,1:T(8,128)}, f32[5,512]{0,1:T(8,128)}, u32[]{:S(2)}, u32[]{:S(2)}) collective-permute-start(f32[5,512]{0,1:T(8,128)} %select_bitcast_fusion.1), channel_id=1, source_target_pairs={{0,15},{1,0},{2,1},{3,2},{4,3},{5,4},{6,5},{7,6},{8,7},{9,8},{10,9... | collective-permute-start | bytes 30728 | tf_op jit(solution)/shard_map/ppermute | solution.py:19
  146.5 24.9 %copy-start.12 = (f32[3,4096]{1,0:T(4,128)S(1)}, f32[3,4096]{1,0:T(4,128)}, u32[]{:S(2)}) copy-start(f32[3,4096]{1,0:T(4,128)} %param.23) | copy-start | bytes 147460
  181.7 185.9 %collective-permute-start.1 = (f32[2,3,128,128]{3,2,1,0:T(8,128)}, f32[2,3,128,128]{3,2,1,0:T(8,128)}, u32[]{:S(2)}, u32[]{:S(2)}) collective-permute-start(f32[2,3,128,128]{3,2,1,0:T(8,128)} %slice.345), channel_id=1, source_target_pairs={{0,15},{1,0},{2,1},{3,2},{4,3},{5,4},{6,5},{7,6},{8,7},{9,8},{10,9... | collective-permute-start | bytes 1179656 | tf_op jit(solution)/shard_map/ppermute | solution.py:19
  195.2 3.8 copy-start.7
  199.1 0.6 copy-start.8
  210.5 3.8 copy-start.7
  214.3 0.6 copy-start.8
  225.7 3.8 copy-start.7
  229.6 0.6 copy-start.8
  241.0 3.8 copy-start.7
  244.9 0.6 copy-start.8
  256.2 3.8 copy-start.7
  260.1 0.6 copy-start.8
  271.5 3.8 copy-start.7
  275.4 0.6 copy-start.8
  286.7 3.8 copy-start.7
  290.6 0.6 copy-start.8
  302.0 3.8 copy-start.7
  305.9 0.6 copy-start.8
  317.3 3.8 copy-start.7
  321.1 0.6 copy-start.8
  332.5 3.8 copy-start.7
  336.4 0.6 copy-start.8
  347.8 3.8 copy-start.7
  351.6 0.6 copy-start.8
  363.0 3.8 copy-start.7
  366.9 0.6 copy-start.8
  367.5 1.7 copy-start.3
  447.0 61.4 %copy-start.1 = (f32[4096,128]{0,1:T(8,128)S(1)}, f32[4096,128]{0,1:T(8,128)}, u32[]{:S(2)}) copy-start(f32[4096,128]{0,1:T(8,128)} %copy-done) | copy-start | bytes 6291460
  447.0 61.4 %copy-start.2 = (f32[4096,128]{0,1:T(8,128)S(1)}, f32[4096,128]{0,1:T(8,128)}, u32[]{:S(2)}) copy-start(f32[4096,128]{0,1:T(8,128)} %get-tuple-element.227) | copy-start | bytes 6291460
  508.4 31.4 %copy-start.6 = (f32[4096,11]{0,1:T(8,128)S(1)}, f32[4096,11]{0,1:T(8,128)}, u32[]{:S(2)}) copy-start(f32[4096,11]{0,1:T(8,128)} %copy-done.5) | copy-start | bytes 540676
  508.4 31.4 %copy-start.10 = (f32[4096,11]{0,1:T(8,128)S(1)}, f32[4096,11]{0,1:T(8,128)}, u32[]{:S(2)}) copy-start(f32[4096,11]{0,1:T(8,128)} %get-tuple-element.225) | copy-start | bytes 540676
  539.8 1.3 copy-start.9
  539.8 1.3 copy-start.18
  539.8 1.3 copy-start.19
where the time goes:
time: 551 us; the launch traced here: 542 us
  other arithmetic  243 us (44%)
  matrix products  142 us (26%)
  local copies, waits for them, and re-layouts  98.1 us (18%)
  waiting for transfers between devices  39.1 us (7%)
  starting transfers between devices  16.4 us (3%)
    dot_general x1, matrix products, per_device(): jnp.einsum('az,rz->ar', stacked_z, potential.reshape(2 * slab_width * ful...  77.7 us
    mul x12, other arithmetic, pair_block(): return jnp.sum((mixed * radial)[None] * separation, axis=3)  69.9 us
    slice x1, local copies, waits for them, and re-layouts, per_device(): slope_zed = sampled[1]  61.4 us
    reduce_sum x12, other arithmetic, pair_block(): return jnp.sum((mixed * radial)[None] * separation, axis=3)  45.8 us
    dot_general x1, matrix products, per_device(): jnp.einsum('ar,az->rz', lifted, rows_z, precision=highest)  41.3 us
    unnamed x3, other arithmetic  31.4 us
    reduce_sum x12, other arithmetic, pair_block(): dist_sq = jnp.sum(separation * separation, axis=0) + soften_sq  24.8 us
    ppermute x4, waiting for transfers between devices, from_behind(): return lax.ppermute(value, axis, pairs)  23.8 us
  transfers between devices with their start and end apart: 6, of which 3 were waited for; matrix products, arithmetic and copies ran while one was open for 38% of the time, Pallas kernels for 0%

commit v1 on v0

v1 whole, which is shorter than its diff:
```python
import functools
import math

import jax
import jax.numpy as jnp
from jax import lax
from jax.experimental import pallas as pl
from jax.experimental.pallas import tpu as pltpu
from jax.sharding import PartitionSpec as P

TILE = 128

high = lax.Precision.HIGH
ewald_beta = 0.35
soften_sq = 0.25
t_scale = 0.13
t_poly = (
    0.2093298660627116,
    0.2140488115708388,
    0.1607995042093057,
    0.2997555766949459,
    -0.16268460574346366,
    0.41880827459241754,
    -0.14005895059197282,
)


def from_behind(value, axis, steps):
    count = lax.axis_size(axis)
    pairs = [(source, (source + steps) % count) for source in range(count)]
    return lax.ppermute(value, axis, pairs)


def phase_tables(rows, length):
    wave_index = jnp.arange(length, dtype=jnp.int32)
    angle = (
        2.0 * math.pi / length * (rows[:, None] * wave_index[None, :] % length).astype(jnp.float32)
    )
    return jnp.cos(angle), jnp.sin(angle)


def forward_matrix(rows, length):
    c, s = phase_tables(rows, length)
    return jnp.stack([jnp.stack([c, -s], axis=1), jnp.stack([s, c], axis=1)])


def inverse_matrix(rows, length):
    c, s = phase_tables(rows, length)
    c, s = c.T, s.T
    return jnp.stack([jnp.stack([c, s], axis=1), jnp.stack([-s, c], axis=1)])


def split(value):
    upper = value.astype(jnp.bfloat16)
    lower = (value - upper.astype(jnp.float32)).astype(jnp.bfloat16)
    return upper, lower


def dot3(a_hi, a_lo, b_hi, b_lo):
    mm = functools.partial(jnp.dot, preferred_element_type=jnp.float32)
    return mm(a_hi, b_hi) + mm(a_lo, b_hi) + mm(a_hi, b_lo)


def banded(cells, base, weights, length):
    gap = cells - base
    if length is not None:
        gap = jnp.where(gap < 0.0, gap + float(length), gap)
    results = [jnp.zeros(gap.shape, jnp.float32) for unused in weights]
    for offset in range(len(weights[0])):
        here = gap == float(offset)
        results = [
            jnp.where(here, group[offset], value) for group, value in zip(weights, results)
        ]
    return results


def cells_of(shape, dim):
    return lax.broadcasted_iota(jnp.int32, shape, dim).astype(jnp.float32)


def spread_kernel(rows_ref, cols_ref, out_ref, hi_ref, lo_ref, *, order, width, full_y, full_z):
    count = rows_ref.shape[1]

    def row(k):
        return rows_ref[k : k + 1, :]

    def col(k):
        return cols_ref[:, k : k + 1]

    padded = -(-width // 8) * 8
    (band_x,) = banded(
        cells_of((padded, count), 0), row(0), [[row(3 + o) for o in range(order)]], None
    )
    (band_y,) = banded(
        cells_of((full_y, count), 0), row(1), [[row(3 + order + o) for o in range(order)]], full_y
    )
    for p in range(width):
        upper, lower = split(band_y * band_x[p : p + 1, :])
        hi_ref[p * full_y : (p + 1) * full_y, :] = upper
        lo_ref[p * full_y : (p + 1) * full_y, :] = lower
    (band_z,) = banded(
        cells_of((count, full_z), 1),
        col(2),
        [[col(3 + 2 * order + o) for o in range(order)]],
        full_z,
    )
    q = 3 + 6 * order
    z_hi, z_lo = split(jnp.concatenate([col(q) * band_z, col(q + 1) * band_z], axis=1))
    total = dot3(hi_ref[...], lo_ref[...], z_hi, z_lo)

    @pl.when(pl.program_id(0) == 0)
    def _():
        out_ref[...] = total

    @pl.when(pl.program_id(0) > 0)
    def _():
        out_ref[...] += total


def gather_kernel(
    cols_ref, grid_ref, pairs_ref, out_ref, hi_ref, lo_ref, *, order, width, full_y, full_z
):
    count = cols_ref.shape[0]

    @pl.when(pl.program_id(0) == 0)
    def _():
        upper, lower = split(grid_ref[...])
        hi_ref[...] = upper
        lo_ref[...] = lower

    def col(k):
        return cols_ref[:, k : k + 1]

    def groups(axis):
        return [
            [col(3 + axis * order + o) for o in range(order)],
            [col(3 + (3 + axis) * order + o) for o in range(order)],
        ]

    plain_x, slope_x = banded(cells_of((count, 128), 1), col(0), groups(0), None)
    plain_y, slope_y = banded(cells_of((count, full_y), 1), col(1), groups(1), full_y)
    plain_z, slope_z = banded(cells_of((count, full_z), 1), col(2), groups(2), full_z)
    q = 3 + 6 * order
    weight_a, weight_b = col(q + 2), col(q + 3)
    tables = hi_ref[...], lo_ref[...]
    plain = dot3(
        *split(jnp.concatenate([weight_a * plain_z, weight_b * plain_z], axis=1)), *tables
    )
    slope = dot3(
        *split(jnp.concatenate([weight_a * slope_z, weight_b * slope_z], axis=1)), *tables
    )
    sum_x = jnp.zeros((count, full_y), jnp.float32)
    sum_y = sum_x
    sum_z = sum_x
    for p in range(width):
        here = slice(p * full_y, (p + 1) * full_y)
        weight, lean = plain_x[:, p : p + 1], slope_x[:, p : p + 1]
        sum_x = sum_x + lean * plain[:, here]
        sum_y = sum_y + weight * plain[:, here]
        sum_z = sum_z + weight * slope[:, here]
    values = (sum_x * plain_y, sum_y * slope_y, sum_z * plain_y)
    for k, value in enumerate(values):
        out_ref[:, k : k + 1] = pairs_ref[:, k : k + 1] + jnp.sum(value, axis=1, keepdims=True)


def pair_kernel(tiles_ref, home_ref, cand_ref, out_ref, *, chunk):
    t = pl.program_id(0)
    slots = tiles_ref.shape[1]
    for start in range(0, TILE, chunk):
        here = slice(start, start + chunk)
        home = [
            jnp.broadcast_to(home_ref[here, k : k + 1], (chunk, TILE)) for k in range(5)
        ]
        total = [jnp.zeros((chunk, TILE), jnp.float32) for unused in range(3)]
        for slot in range(slots):
            k = tiles_ref[t, slot]
            near = cand_ref[k]
            gaps = [home[d] - near[d : d + 1, :] for d in range(3)]
            dist_sq = gaps[0] * gaps[0] + gaps[1] * gaps[1] + gaps[2] * gaps[2] + soften_sq
            inverse = lax.rsqrt(dist_sq)
            t_value = pl.reciprocal(1.0 + t_scale * (dist_sq * inverse))
            poly = t_poly[-1]
            for factor in t_poly[-2::-1]:
                poly = poly * t_value + factor
            bracket = poly * (t_value * inverse) + 2.0 * ewald_beta / math.sqrt(math.pi)
            decay = jnp.exp2(dist_sq * (-ewald_beta * ewald_beta * math.log2(math.e)))
            mixed = home[3] * near[3:4, :] + home[4] * near[4:5, :]
            weight = (mixed * decay) * (bracket * (inverse * inverse))
            total = [value + weight * gap for value, gap in zip(total, gaps)]
        for d in range(3):
            out_ref[here, d : d + 1] = jnp.sum(total[d], axis=1, keepdims=True)


def per_device(
    charge_a,
    charge_b,
    coupling,
    positions,
    grid_base,
    spline,
    spline_slope,
    influence,
    pair_tiles,
    ghost_lists,
):
    group_size = lax.axis_size("px")
    me_index = lax.axis_index("px")
    atom_count = charge_a.shape[0]
    full_x, slab_y, full_z = influence.shape
    full_y = slab_y * group_size
    planes = full_x // group_size
    order = spline.shape[1]
    width = planes + order - 1
    cells = width * full_y
    weight_b = coupling[0]
    scale = 1.0 / (full_x * full_y * full_z)

    packet = jnp.concatenate([positions, charge_a[None], charge_b[None]], axis=0)
    by_atom = packet.T
    from_left = from_behind(jnp.take(by_atom, ghost_lists[0], axis=0).T, "px", 1)
    from_right = from_behind(jnp.take(by_atom, ghost_lists[1], axis=0).T, "px", -1)

    base = jnp.stack([grid_base[0] - me_index * planes, grid_base[1], grid_base[2]])
    rows = jnp.concatenate(
        [
            base.astype(jnp.float32),
            spline.reshape(3 * order, atom_count),
            spline_slope.reshape(3 * order, atom_count),
            charge_a[None],
            charge_b[None],
            (-scale * (1.0 - weight_b) * charge_a)[None],
            (-scale * weight_b * charge_b)[None],
        ],
        axis=0,
    )
    rows = jnp.pad(rows, ((0, -rows.shape[0] % 8), (0, 0)))
    fields = rows.shape[0]
    cols = rows.T

    block = min(512, atom_count)
    sizes = dict(order=order, width=width, full_y=full_y, full_z=full_z)
    spread = pl.pallas_call(
        functools.partial(spread_kernel, **sizes),
        grid=(atom_count // block,),
        in_specs=[
            pl.BlockSpec((fields, block), lambda i: (0, i)),
            pl.BlockSpec((block, fields), lambda i: (i, 0)),
        ],
        out_specs=pl.BlockSpec((cells, 2 * full_z), lambda i: (0, 0)),
        out_shape=jax.ShapeDtypeStruct((cells, 2 * full_z), jnp.float32),
        scratch_shapes=[pltpu.VMEM((cells, block), jnp.bfloat16)] * 2,
        compiler_params=pltpu.CompilerParams(vmem_limit_bytes=56 << 20),
        cost_estimate=pl.CostEstimate(
            flops=12 * atom_count * cells * full_z, bytes_accessed=4 << 20, transcendentals=0
        ),
        name="spread",
    )(rows, cols)

    slab_rows = (
        jnp.arange(group_size, dtype=jnp.int32)[:, None] * planes
        + jnp.arange(width, dtype=jnp.int32)[None, :]
    ).reshape(-1) % full_x
    range_y = jnp.arange(full_y, dtype=jnp.int32)
    range_z = jnp.arange(full_z, dtype=jnp.int32)
    along_z = forward_matrix(range_z, full_z).reshape(2 * full_z, 2, full_z)
    waves = jnp.einsum("pyc,cdk->dpyk", spread.reshape(width, full_y, 2 * full_z), along_z, precision=high)
    waves = jnp.einsum("dpyk,dyew->epwk", waves, forward_matrix(range_y, full_y), precision=high)
    columns = lax.all_to_all(waves, "px", split_axis=2, concat_axis=1, tiled=True)
    columns = jnp.einsum("dxwk,dxeu->euwk", columns, forward_matrix(slab_rows, full_x), precision=high)
    columns = columns * influence[None]
    columns = jnp.einsum("duwk,duex->exwk", columns, inverse_matrix(slab_rows, full_x), precision=high)
    returned = lax.all_to_all(columns, "px", split_axis=1, concat_axis=2, tiled=True)
    returned = jnp.einsum("dpwk,dwey->ekpy", returned, inverse_matrix(range_y, full_y), precision=high)
    potential = jnp.einsum("dkpy,dkez->ezpy", returned, inverse_matrix(range_z, full_z), precision=high)
    potential = potential.reshape(2 * full_z, cells)

    shift = jnp.where(me_index == 0, -float(full_x), 0.0)
    from_left = jnp.concatenate([from_left[:1] + shift, from_left[1:]], axis=0)
    shift = jnp.where(me_index == group_size - 1, float(full_x), 0.0)
    from_right = jnp.concatenate([from_right[:1] + shift, from_right[1:]], axis=0)
    candidates = jnp.concatenate([packet, from_left, from_right], axis=1)
    cand_tiles = candidates.reshape(5, -1, TILE).transpose(1, 0, 2)
    cand_tiles = jnp.pad(cand_tiles, ((0, 0), (0, 3), (0, 0)))
    home = jnp.concatenate(
        [
            positions,
            ((1.0 - weight_b) * charge_a)[None],
            (weight_b * charge_b)[None],
            jnp.zeros((3, atom_count), jnp.float32),
        ],
        axis=0,
    ).T
    tile_count, slots = pair_tiles.shape
    pair_work = tile_count * slots * TILE * TILE
    pairs = pl.pallas_call(
        functools.partial(pair_kernel, chunk=32),
        grid_spec=pltpu.PrefetchScalarGridSpec(
            num_scalar_prefetch=1,
            grid=(tile_count,),
            in_specs=[
                pl.BlockSpec((TILE, 8), lambda i, tiles: (i, 0)),
                pl.BlockSpec(cand_tiles.shape, lambda i, tiles: (0, 0, 0)),
            ],
            out_specs=pl.BlockSpec((TILE, 8), lambda i, tiles: (i, 0)),
        ),
        out_shape=jax.ShapeDtypeStruct((atom_count, 8), jnp.float32),
        cost_estimate=pl.CostEstimate(
            flops=50 * pair_work, bytes_accessed=4 << 20, transcendentals=3 * pair_work
        ),
        name="pairs",
    )(pair_tiles, home, cand_tiles)

    block = min(256, atom_count)
    forces = pl.pallas_call(
        functools.partial(gather_kernel, **sizes),
        grid=(atom_count // block,),
        in_specs=[
            pl.BlockSpec((block, fields), lambda i: (i, 0)),
            pl.BlockSpec((2 * full_z, cells), lambda i: (0, 0)),
            pl.BlockSpec((block, 8), lambda i: (i, 0)),
        ],
        out_specs=pl.BlockSpec((block, 8), lambda i: (i, 0)),
        out_shape=jax.ShapeDtypeStruct((atom_count, 8), jnp.float32),
        scratch_shapes=[pltpu.VMEM((2 * full_z, cells), jnp.bfloat16)] * 2,
        compiler_params=pltpu.CompilerParams(vmem_limit_bytes=56 << 20),
        cost_estimate=pl.CostEstimate(
            flops=24 * atom_count * cells * full_z, bytes_accessed=6 << 20, transcendentals=0
        ),
        name="gather",
    )(cols, potential, pairs)
    return forces[:, :3].T


def solution(mesh):
    placed = (
        P(("win", "px")),
        P(("win", "px")),
        P("win"),
        P(None, ("win", "px")),
        P(None, ("win", "px")),
        P(None, None, ("win", "px")),
        P(None, None, ("win", "px")),
        P(None, "px", None),
        P(("win", "px"), None),
        P(None, ("win", "px")),
    )
    return jax.shard_map(
        per_device, mesh=mesh, in_specs=placed, out_specs=P(None, ("win", "px")), check_vma=False
    )
```

time: 551 us -> 225 us (0.41); the launches traced: 542 us -> 224 us
  other arithmetic: 243 us -> 18.5 us
  matrix products: 142 us -> 7.16 us
  Pallas kernels: 0 us -> 112 us
  local copies, waits for them, and re-layouts: 98.1 us -> 32.8 us
    dot_general x26 -> x6, matrix products: 142 us -> 7.16 us  [the longest x1 2.76 us: per_device(): jnp.einsum('pyc,cdk->dpyk', spread.reshape(width, full_y, 2 * full_z), al...]
    pallas_call x0 -> x3, Pallas kernels: none -> 112 us  [the longest x1 47.4 us: per_device(): pl.pallas_call(functools.partial(pair_kernel, chunk=32), grid_spec=pltpu....]
    mul x28 -> x3, other arithmetic: 106 us -> 2.67 us  [the longest x1 1.34 us: per_device(): (1.0 - weight_b) * charge_a]
    reduce_sum x24 -> x0, other arithmetic: 70.7 us -> none  [the longest x12 45.8 us: pair_block(): return jnp.sum((mixed * radial)[None] * separation, axis=3)]
    slice x59 -> x4, local copies, waits for them, and re-layouts: 66.9 us -> 2.18 us  [the longest x1 0.86 us: per_device(): grid_base[1]]
    unnamed x3 -> x0, other arithmetic: 31.4 us -> none
    select_n x30 -> x3, other arithmetic: 12.2 us -> 1.96 us  [the longest x1 0.7 us: per_device(): (jnp.arange(group_size, dtype=jnp.int32)[:, None] * planes + jnp.arange(w...]
    ppermute x4 -> x2, waiting for transfers between devices: 23.8 us -> 14.2 us  [from_behind(): return lax.ppermute(value, axis, pairs)]
  transfers between devices with their start and end apart: 6 -> 4, of which waited for: 3 -> 2; matrix products, arithmetic and copies ran while one was open for 38% -> 12% of each run, Pallas kernels for 0% -> 21%
where the time goes in v1:
time: 225 us; the launch traced here: 224 us
  Pallas kernels  112 us (50%)
  waiting for transfers between devices  39.1 us (17%)
  local copies, waits for them, and re-layouts  32.8 us (15%)
  other arithmetic  18.5 us (8%)
  starting transfers between devices  13.7 us (6%)
  matrix products  7.16 us (3%)
    pallas_call x1, Pallas kernels, per_device(): pl.pallas_call(functools.partial(pair_kernel, chunk=32), grid_spec=pltpu....  47.4 us
    pallas_call x1, Pallas kernels, per_device(): pl.pallas_call(functools.partial(gather_kernel, **sizes), grid=(atom_coun...  44.9 us
    all_to_all x1, waiting for transfers between devices, per_device(): lax.all_to_all(waves, 'px', split_axis=2, concat_axis=1, tiled=True)  24.8 us
    pallas_call x1, Pallas kernels, per_device(): pl.pallas_call(functools.partial(spread_kernel, **sizes), grid=(atom_coun...  19.6 us
    ppermute x2, waiting for transfers between devices, from_behind(): return lax.ppermute(value, axis, pairs)  14.2 us
    all_to_all x1, starting transfers between devices, per_device(): lax.all_to_all(waves, 'px', split_axis=2, concat_axis=1, tiled=True)  6.28 us
    unnamed x34, local copies, waits for them, and re-layouts  5.68 us
    all_to_all x1, starting transfers between devices, per_device(): lax.all_to_all(columns, 'px', split_axis=1, concat_axis=2, tiled=True)  4.54 us
  transfers between devices with their start and end apart: 4, of which 2 were waited for; matrix products, arithmetic and copies ran while one was open for 12% of the time, Pallas kernels for 21%

profile of v1, /device:TPU:20, one launch (start us, length us, event | category | flops | bytes accessed | tf_op | source)
XLA Modules:
  0.0 224.1 jit_solution(14662734111929933159)
XLA Ops:
  0.0 0.9 fusion.50
  0.9 0.9 fusion.48
  2.5 0.9 slice.30
  3.3 0.9 slice_subtract_fusion
  4.2 1.0 reshape.383
  5.2 1.0 reshape.384
  6.2 1.3 broadcast_multiply_fusion.1
  7.6 1.3 broadcast_multiply_fusion
  8.9 0.7 concatenate.18
  9.7 0.6 copy.153
  10.3 0.6 copy.228
  11.0 1.5 pad_bitcast_fusion.cols_ref
  12.5 0.7 fusion.22
  13.4 0.8 pad.8.clone.rows_ref
  14.2 19.6 %spread.1 = f32[1408,256]{1,0:T(8,128)} custom-call(f32[32,4096]{1,0:T(8,128)} %pad.8.clone.rows_ref, f32[4096,32]{1,0:T(8,128)} %pad_bitcast_fusion.cols_ref), custom_call_target="tpu_custom_call" | custom-call | flops 8858370048 | bytes 4194304 | tf_op jit(solution)/shard_map/spread/pallas_call | solution.py:242
  33.8 2.8 %convolution_bitcast_fusion.4 = f32[2,11,128,128,1]{2,3,0,1,4:T(8,128)S(1)} fusion(f32[256,2,128,1]{2,0,1,3:T(8,128)S(1)} %bitcast.141, f32[11,128,256,1]{2,1,3,0:T(8,128)} %bitcast.140), kind=kOutput, calls=%fused_computation.7 | convolution fusion | flops 553648128 | bytes 3145728 | tf_op jit(solution)/shard_map/pyc,cdk->dpyk/dot_general | solution.py:266
  36.6 0.8 convolution_bitcast_fusion.3
  37.4 2.2 copy.161
  39.6 6.3 %all-to-all-start = ((f32[2,11,128,128]{3,0,1,2:T(2,128)}), f32[2,11,128,128]{3,0,1,2:T(2,128)S(1)}, u32[]{:S(2)}, u32[]{:S(2)}) async-start(f32[2,11,128,128]{3,0,1,2:T(2,128)} %copy.161), calls=%async_computation | async-start | bytes 2883584 | tf_op jit(solution)/shard_map/all_to_all | solution.py:268
  46.0 0.7 add.227
  46.7 0.9 copy.165
  47.6 0.7 pad_maximum_fusion.6
  48.3 1.5 copy.175
  49.8 0.7 and_select_fusion
  50.5 0.4 fusion.44
  51.0 0.8 maximum_bitcast_fusion.4
  51.7 0.4 fusion.47
  52.2 0.8 maximum_bitcast_fusion.6
  53.0 0.6 fusion.55
  53.5 0.5 compare_and_fusion.1
  54.1 0.6 compare_select_fusion.1
  54.7 24.8 %all-to-all-done = f32[2,11,128,128]{3,0,1,2:T(2,128)S(1)} async-done(((f32[2,11,128,128]{3,0,1,2:T(2,128)}), f32[2,11,128,128]{3,0,1,2:T(2,128)S(1)}, u32[]{:S(2)}, u32[]{:S(2)}) %all-to-all-start) | async-done | bytes 1441824 | tf_op jit(solution)/shard_map/all_to_all | solution.py:268
  79.5 0.2 copy.232
  79.8 0.9 copy-done
  80.8 1.2 fusion.9
  82.0 0.8 convolution_bitcast_fusion.2
  82.8 1.5 copy.166
  84.3 4.5 %all-to-all-start.1 = ((f32[2,176,8,128]{3,2,0,1:T(8,128)}), f32[2,176,8,128]{3,2,0,1:T(8,128)S(1)}, u32[]{:S(2)}, u32[]{:S(2)}) async-start(f32[2,176,8,128]{3,2,0,1:T(8,128)} %copy.166), calls=%async_computation.1 | async-start | bytes 2883584 | tf_op jit(solution)/shard_map/all_to_all | solution.py:272
  88.9 1.3 pad_clamp_fusion.1
  90.1 1.8 gather_fusion
  91.9 1.7 copy.176
  93.6 1.3 select_bitcast_fusion.1
  95.0 0.7 compare_select_fusion
  95.7 0.6 pad_clamp_fusion
  96.3 1.8 gather_fusion.1
  98.1 1.1 copy.177
  99.1 0.7 compare_and_fusion
  99.8 2.8 %collective-permute-start.1 = (f32[5,512]{1,0:T(8,128)S(1)}, f32[5,512]{1,0:T(8,128)S(1)}, u32[]{:S(2)}, u32[]{:S(2)}) collective-permute-start(f32[5,512]{1,0:T(8,128)S(1)} %select_bitcast_fusion), channel_id=1, source_target_pairs={{0,15},{1,0},{2,1},{3,2},{4,3},{5,4},{6,5},{7,6},{8,7},{9,8},{10,9... | collective-permute-start | bytes 30728 | tf_op jit(solution)/shard_map/ppermute | solution.py:31
  102.7 1.0 maximum_maximum_fusion
  103.7 1.0 fusion.54
  104.7 1.4 copy.179.tiles_ref
  106.1 2.0 copy.174
  108.1 14.2 %collective-permute-done = f32[5,512]{1,0:T(8,128)} collective-permute-done((f32[5,512]{1,0:T(8,128)}, f32[5,512]{1,0:T(8,128)}, u32[]{:S(2)}, u32[]{:S(2)}) %collective-permute-start) | collective-permute-done | bytes 10272 | tf_op jit(solution)/shard_map/ppermute | solution.py:31
  122.3 0.7 slice.43
  123.0 0.7 slice_add_fusion.1
  123.8 0.7 pad.9.cand_ref
  124.6 47.4 %pairs.1.pairs_ref = f32[4096,8]{1,0:T(8,128)} custom-call(s32[32,12]{1,0:T(8,128)} %copy.179.tiles_ref, f32[4096,8]{1,0:T(8,128)} %bitcast.138, f32[40,8,128]{2,1,0:T(8,128)} %pad.9.cand_ref), custom_call_target="tpu_custom_call" | custom-call | flops 314572800 | bytes 4194304 | tf_op jit(solution)/shard_map/pairs/pallas_call | solution.py:295
  171.9 0.8 convolution_bitcast_fusion.1
  172.7 0.8 convolution_bitcast_fusion
  173.6 0.9 copy.206
  174.4 1.7 copy.231
  176.1 44.9 %gather.11 = f32[4096,8]{1,0:T(8,128)} custom-call(f32[4096,32]{1,0:T(8,128)} %pad_bitcast_fusion.cols_ref, f32[256,1408]{1,0:T(8,128)} %bitcast.139, f32[4096,8]{1,0:T(8,128)} %pairs.1.pairs_ref), custom_call_target="tpu_custom_call" | custom-call | flops 17716740096 | bytes 6291456 | tf_op jit(solution)/shard_map/gather/pallas_call | solution.py:314
  221.1 1.7 slice_bitcast_fusion
  222.8 1.2 copy.181
  (44 shorter events, 0.8 us)
Async XLA Ops:
  0.0 8.9 %copy-start.8 = (f32[4096]{0:T(1024)S(1)}, f32[4096]{0:T(1024)}, u32[]{:S(2)}) copy-start(f32[4096]{0:T(1024)} %param.12) | copy-start | bytes 49156
  0.0 8.9 %copy-start.9 = (f32[4096]{0:T(1024)S(1)}, f32[4096]{0:T(1024)}, u32[]{:S(2)}) copy-start(f32[4096]{0:T(1024)} %param.13) | copy-start | bytes 49156
  10.9 1.5 copy-start.11
  10.9 1.5 copy-start.12
  11.0 1.5 copy-start.13
  39.6 7.0 %copy-start.7 = (f32[128,8,128]{2,1,0:T(8,128)S(1)}, f32[128,8,128]{2,1,0:T(8,128)}, u32[]{:S(2)}) copy-start(f32[128,8,128]{2,1,0:T(8,128)} %param.19) | copy-start | bytes 1572868
  39.6 7.9 %copy-start.5 = (f32[3,4096]{1,0:T(4,128)S(1)}, f32[3,4096]{1,0:T(4,128)}, u32[]{:S(2)}) copy-start(f32[3,4096]{1,0:T(4,128)} %param.15) | copy-start | bytes 147460
  39.6 39.8 %all-to-all-start = ((f32[2,11,128,128]{3,0,1,2:T(2,128)}), f32[2,11,128,128]{3,0,1,2:T(2,128)S(1)}, u32[]{:S(2)}, u32[]{:S(2)}) async-start(f32[2,11,128,128]{3,0,1,2:T(2,128)} %copy.161), calls=%async_computation | async-start | bytes 2883584 | tf_op jit(solution)/shard_map/all_to_all | solution.py:268
  49.8 3.1 %copy-start.14 = (s32[2,512]{1,0:T(2,128)S(1)}, s32[2,512]{1,0:T(2,128)}, u32[]{:S(2)}) copy-start(s32[2,512]{1,0:T(2,128)} %param.21) | copy-start | bytes 12292
  79.7 1.0 copy-start
  79.7 1.1 copy-start.1
  79.7 1.1 copy-start.2
  80.8 1.2 copy-start.3
  80.8 1.2 copy-start.4
  84.3 87.6 %all-to-all-start.1 = ((f32[2,176,8,128]{3,2,0,1:T(8,128)}), f32[2,176,8,128]{3,2,0,1:T(8,128)S(1)}, u32[]{:S(2)}, u32[]{:S(2)}) async-start(f32[2,176,8,128]{3,2,0,1:T(8,128)} %copy.166), calls=%async_computation.1 | async-start | bytes 2883584 | tf_op jit(solution)/shard_map/all_to_all | solution.py:272
  94.9 27.4 %collective-permute-start = (f32[5,512]{1,0:T(8,128)}, f32[5,512]{1,0:T(8,128)}, u32[]{:S(2)}, u32[]{:S(2)}) collective-permute-start(f32[5,512]{1,0:T(8,128)} %select_bitcast_fusion.1), channel_id=1, source_target_pairs={{0,1},{1,2},{2,3},{3,4},{4,5},{5,6},{6,7},{7,8},{8,9},{9,10},{10,1... | collective-permute-start | bytes 30728 | tf_op jit(solution)/shard_map/ppermute | solution.py:31
  99.8 23.2 %collective-permute-start.1 = (f32[5,512]{1,0:T(8,128)S(1)}, f32[5,512]{1,0:T(8,128)S(1)}, u32[]{:S(2)}, u32[]{:S(2)}) collective-permute-start(f32[5,512]{1,0:T(8,128)S(1)} %select_bitcast_fusion), channel_id=1, source_target_pairs={{0,15},{1,0},{2,1},{3,2},{4,3},{5,4},{6,5},{7,6},{8,7},{9,8},{10,9... | collective-permute-start | bytes 30728 | tf_op jit(solution)/shard_map/ppermute | solution.py:31
  103.7 20.1 %copy-start.6 = (f32[3,4096]{1,0:T(4,128)S(1)}, f32[3,4096]{1,0:T(4,128)}, u32[]{:S(2)}) copy-start(f32[3,4096]{1,0:T(4,128)} %param.15) | copy-start | bytes 147460
  103.7 20.1 %copy-start.10 = (f32[4096]{0:T(1024)S(1)}, f32[4096]{0:T(1024)}, u32[]{:S(2)}) copy-start(f32[4096]{0:T(1024)} %param.13) | copy-start | bytes 49156
